TPU v7x, 32 devices: a whole 2x2x4 slice. The times are simulated.
32 devices in a mesh: grp: 2 (over x), chan: 16 (over z, y, core).
Axes of the slice: x: 2, y: 2, z: 4, core: 2. Of those that a mesh axis runs over, the one named last changes fastest.
Arguments:
- voltages: bfloat16 [8, 16384, 2048], P('grp', 'chan'), parts along dimension 0, may hold values from -6 to 6
- delay_step: int32 [16384], replicated, may hold values from 0 to 1048575
- trials: int32 [256], replicated, may hold values from 0 to 2047
Outputs:
- spectra: float32 [48, 2, 8, 256], P('chan', None, 'grp'), parts along dimension 2
- power: float32 [8, 256], P('grp', 'chan'), parts along dimension 0
There are 2 independent parts, one for each index of `grp`. A program takes and returns all parts, laid end to end along the dimension named above; an argument that names none is the same for every part. Nothing has to cross between parts.
All inputs are finite; a program needn't handle non-finite values.
Results may differ from a plain program's by a relative error of at most 0.0037.
Values may be sent and summed in bfloat16 or wider, within the bound.
No kernel may reach another device: no remote copies, remote signals or barrier semaphores. Data moves between devices by JAX's collectives and lax.ppermute only.
A program may use at most 64 MiB of HBM per device.

v0:
```python
import math
import jax
import jax.numpy as jnp
from jax import lax
from jax.sharding import PartitionSpec as P

SUBSTEPS = 512
SPIN_DEV = 3


def build_table(samples, bins):
    times = jnp.arange(samples, dtype=jnp.int32)
    frequency = jnp.arange(bins, dtype=jnp.int32)
    phase_index = times[:, None] * frequency[None, :] % samples
    angles = phase_index.astype(jnp.float32) * (2.0 * math.pi / samples)
    return jnp.concatenate([jnp.cos(angles), -jnp.sin(angles)], axis=1).astype(jnp.bfloat16)


def make_phases(spin_bin, delay_step, trials, modulus):
    chan_phase = spin_bin * delay_step % modulus
    phase_index = chan_phase[:, None] * trials[None, :] % modulus
    angles = phase_index.astype(jnp.float32) * (2.0 * math.pi / modulus)
    return jnp.concatenate([jnp.cos(angles), jnp.sin(angles)], axis=1)


def dedisperse(pair_rows, spin_bin, delay_step, trials, modulus, beam_count, chan_scale):
    rows_wide = pair_rows.astype(jnp.float32)
    half_count = trials.shape[0] // 2
    pieces = []
    for half_index in range(2):
        trial_half = trials[half_index * half_count : (half_index + 1) * half_count]
        phases = make_phases(spin_bin, delay_step, trial_half, modulus)
        product = jnp.dot(
            rows_wide, phases, precision=lax.Precision.HIGHEST, preferred_element_type=jnp.float32
        )
        real_rows = product[:beam_count]
        imag_rows = product[beam_count:]
        real_out = real_rows[:, :half_count] - imag_rows[:, half_count:]
        imag_out = real_rows[:, half_count:] + imag_rows[:, :half_count]
        pieces.append(jnp.stack([real_out, imag_out]))
    return jnp.concatenate(pieces, axis=2) * chan_scale


def per_device(voltages, delay_step, trials):
    beam_count, local_chan, samples = voltages.shape
    modulus = samples * SUBSTEPS
    chan_count = lax.axis_size("chan")
    bins_total = SPIN_DEV * chan_count
    all_chan = delay_step.shape[0]
    chan_scale = 1.0 / math.sqrt(all_chan)
    dft_table = build_table(samples, bins_total)
    spectrum = lax.dot_general(
        dft_table, voltages, (((0,), (2,)), ((), ())), preferred_element_type=jnp.float32
    )
    spectrum = (spectrum * (1.0 / math.sqrt(samples))).astype(jnp.bfloat16)
    spectrum = spectrum.reshape(2, bins_total, beam_count, local_chan)
    regrouped = lax.all_to_all(spectrum, "chan", split_axis=1, concat_axis=3, tiled=True)
    first_bin = lax.axis_index("chan") * SPIN_DEV

    def one_bin(offset):
        pair_rows = lax.dynamic_index_in_dim(regrouped, offset, axis=1, keepdims=False).reshape(
            2 * beam_count, all_chan
        )
        return dedisperse(
            pair_rows, first_bin + offset, delay_step, trials, modulus, beam_count, chan_scale
        )

    spectra = lax.map(one_bin, jnp.arange(SPIN_DEV, dtype=jnp.int32))
    power_part = jnp.sum(spectra * spectra, axis=(0, 1)) / bins_total
    power_out = lax.psum_scatter(power_part, "chan", scatter_dimension=1, tiled=True)
    return (spectra, power_out)


def solution(mesh):
    return jax.shard_map(
        per_device,
        mesh=mesh,
        in_specs=(P("grp", "chan", None), P(), P()),
        out_specs=(P("chan", None, "grp", None), P("grp", "chan")),
        check_vma=False,
    )
```

profile of v0, /device:TPU:0, one launch (start us, length us, event | category | flops | bytes accessed | tf_op | source)
XLA Modules:
  0.0 369.8 jit_solution(14272384766015729863)
XLA Ops:
  7.2 1.6 negate_convert_fusion
  8.8 0.0 copy-start
  8.8 0.0 copy-start.1
  8.8 11.1 %multiply_convert_fusion = bf16[96,4,1024]{2,0,1:T(8,128)(2,1)S(1)} fusion(bf16[4,1024,2048]{2,1,0:T(8,128)(2,1)} %param.5, bf16[2048,48]{0,1:T(8,128)(2,1)S(1)} %get-tuple-element.121, bf16[2048,48]{0,1:T(8,128)(2,1)S(1)} %get-tuple-element.122), kind=kOutput, calls=%fused_computation.47 | convolution fusion | flops 1612185600 | bytes 17956864 | tf_op jit(solution)/shard_map/dot_general | solution.py:52
  19.9 1.5 copy.9
  21.4 7.4 %all-to-all-start = ((bf16[2,48,4,1024]{3,2,0,1:T(4,128)(2,1)}), bf16[2,48,4,1024]{3,2,0,1:T(4,128)(2,1)S(1)}, u32[]{:S(2)}, u32[]{:S(2)}) async-start(bf16[2,48,4,1024]{3,2,0,1:T(4,128)(2,1)} %copy.9), calls=%async_computation | async-start | bytes 1572864 | tf_op jit(solution)/shard_map/all_to_all | solution.py:57
  28.8 0.0 reduce-scatter.4.cloned.1.call-start
  28.8 18.6 %all-to-all-done = bf16[2,48,4,1024]{3,2,0,1:T(4,128)(2,1)S(1)} async-done(((bf16[2,48,4,1024]{3,2,0,1:T(4,128)(2,1)}), bf16[2,48,4,1024]{3,2,0,1:T(4,128)(2,1)S(1)}, u32[]{:S(2)}, u32[]{:S(2)}) %all-to-all-start) | async-done | bytes 786464 | tf_op jit(solution)/shard_map/all_to_all | solution.py:57
  47.5 0.4 copy.11
  47.9 0.6 all_to_all.16
  48.5 0.0 copy-done
  48.5 0.0 copy-done.1
  48.5 256.2 %while.12 = (s32[]{:T(128)}, f32[3,2,4,256]{3,2,1,0:T(4,128)S(1)}, s32[3]{0:T(128)S(1)}, bf16[2,3,4,16384]{3,2,1,0:T(4,128)(2,1)S(1)}, s32[]{:T(128)}, /*index=5...) while((s32[]{:T(128)}, f32[3,2,4,256]{3,2,1,0:T(4,128)S(1)}, s32[3]{0:T(128)S(1)}, ...), condition=%wide.region_1.2_spmd, body=%wide.region_0.1_spmd.sunk | while | flops 872620032 | bytes 68955304 | solution.py:68
  48.7 0.6 dynamic_slice.18
  51.2 0.1 constant_dynamic-slice_fusion.2
  51.3 0.1 reshape.66
  52.1 67.4 %fusion.55 = (f32[16384,128]{1,0:T(8,128)S(1)}, f32[16384,128]{1,0:T(8,128)S(1)}, f32[16384,128]{1,0:T(8,128)}, f32[16384,128]{1,0:T(8,128)}) fusion(s32[128]{0:T(128)S(1)} %get-tuple-element.178, s32[16384]{0:T(1024)S(1)} %add_select_fusion.5, s32[128]{0:T(128)S(1)} %get-tuple-element.179), kind=kLoop, calls=%fused_computation.27.clone.1 | loop fusion | flops 58720256 | bytes 33620992 | tf_op jit(solution)/shard_map/while/body/eval_jaxpr/cos | solution.py:23
  119.5 8.9 %fusion.58 = f32[8,256]{1,0:T(8,128)S(1)} fusion(bf16[8,16384]{1,0:T(8,128)(2,1)S(1)} %reshape.66, f32[16384,128]{1,0:T(8,128)} %get-tuple-element.184, f32[16384,128]{1,0:T(8,128)} %get-tuple-element.185), kind=kOutput, calls=%fused_computation.4.clone.1 | convolution fusion | flops 406847488 | bytes 17047552 | tf_op jit(solution)/shard_map/while/body/eval_jaxpr/dot_general | solution.py:33
  128.5 5.5 %fusion.56 = f32[8,256]{1,0:T(8,128)S(1)} fusion(bf16[8,16384]{1,0:T(8,128)(2,1)S(1)} %reshape.66, f32[16384,128]{1,0:T(8,128)S(1)} %get-tuple-element.180, f32[16384,128]{1,0:T(8,128)S(1)} %get-tuple-element.181), kind=kOutput, calls=%fused_computation.clone.1 | convolution fusion | flops 406847488 | bytes 17047552 | tf_op jit(solution)/shard_map/while/body/eval_jaxpr/dot_general | solution.py:33
  134.1 0.6 dynamic_slice.18
  136.6 0.1 constant_dynamic-slice_fusion.2
  136.7 0.1 reshape.66
  137.4 67.4 %fusion.55 = (f32[16384,128]{1,0:T(8,128)S(1)}, f32[16384,128]{1,0:T(8,128)S(1)}, f32[16384,128]{1,0:T(8,128)}, f32[16384,128]{1,0:T(8,128)}) fusion(s32[128]{0:T(128)S(1)} %get-tuple-element.178, s32[16384]{0:T(1024)S(1)} %add_select_fusion.5, s32[128]{0:T(128)S(1)} %get-tuple-element.179), kind=kLoop, calls=%fused_computation.27.clone.1 | loop fusion | flops 58720256 | bytes 33620992 | tf_op jit(solution)/shard_map/while/body/eval_jaxpr/cos | solution.py:23
  204.9 8.9 %fusion.58 = f32[8,256]{1,0:T(8,128)S(1)} fusion(bf16[8,16384]{1,0:T(8,128)(2,1)S(1)} %reshape.66, f32[16384,128]{1,0:T(8,128)} %get-tuple-element.184, f32[16384,128]{1,0:T(8,128)} %get-tuple-element.185), kind=kOutput, calls=%fused_computation.4.clone.1 | convolution fusion | flops 406847488 | bytes 17047552 | tf_op jit(solution)/shard_map/while/body/eval_jaxpr/dot_general | solution.py:33
  213.8 5.5 %fusion.56 = f32[8,256]{1,0:T(8,128)S(1)} fusion(bf16[8,16384]{1,0:T(8,128)(2,1)S(1)} %reshape.66, f32[16384,128]{1,0:T(8,128)S(1)} %get-tuple-element.180, f32[16384,128]{1,0:T(8,128)S(1)} %get-tuple-element.181), kind=kOutput, calls=%fused_computation.clone.1 | convolution fusion | flops 406847488 | bytes 17047552 | tf_op jit(solution)/shard_map/while/body/eval_jaxpr/dot_general | solution.py:33
  219.4 0.6 dynamic_slice.18
  221.9 0.1 constant_dynamic-slice_fusion.2
  222.0 0.1 reshape.66
  222.8 67.4 %fusion.55 = (f32[16384,128]{1,0:T(8,128)S(1)}, f32[16384,128]{1,0:T(8,128)S(1)}, f32[16384,128]{1,0:T(8,128)}, f32[16384,128]{1,0:T(8,128)}) fusion(s32[128]{0:T(128)S(1)} %get-tuple-element.178, s32[16384]{0:T(1024)S(1)} %add_select_fusion.5, s32[128]{0:T(128)S(1)} %get-tuple-element.179), kind=kLoop, calls=%fused_computation.27.clone.1 | loop fusion | flops 58720256 | bytes 33620992 | tf_op jit(solution)/shard_map/while/body/eval_jaxpr/cos | solution.py:23
  290.2 8.9 %fusion.58 = f32[8,256]{1,0:T(8,128)S(1)} fusion(bf16[8,16384]{1,0:T(8,128)(2,1)S(1)} %reshape.66, f32[16384,128]{1,0:T(8,128)} %get-tuple-element.184, f32[16384,128]{1,0:T(8,128)} %get-tuple-element.185), kind=kOutput, calls=%fused_computation.4.clone.1 | convolution fusion | flops 406847488 | bytes 17047552 | tf_op jit(solution)/shard_map/while/body/eval_jaxpr/dot_general | solution.py:33
  299.1 5.5 %fusion.56 = f32[8,256]{1,0:T(8,128)S(1)} fusion(bf16[8,16384]{1,0:T(8,128)(2,1)S(1)} %reshape.66, f32[16384,128]{1,0:T(8,128)S(1)} %get-tuple-element.180, f32[16384,128]{1,0:T(8,128)S(1)} %get-tuple-element.181), kind=kOutput, calls=%fused_computation.clone.1 | convolution fusion | flops 406847488 | bytes 17047552 | tf_op jit(solution)/shard_map/while/body/eval_jaxpr/dot_general | solution.py:33
  304.7 0.0 copy-start.2
  304.8 0.8 copy.13
  305.6 0.0 reduce-scatter.4.cloned.1.call-update
  305.6 56.0 %reduce-scatter.4.cloned.1.call-done = f32[16,4]{1,0:T(8,128)} async-done(((f32[256,4]{1,0:T(8,128)}), f32[16,4]{1,0:T(8,128)}) %reduce-scatter.4.cloned.1.call-update) | async-done | bytes 272
  361.6 1.3 copy.14
  362.9 0.0 copy-done.2
  (22 shorter events, 0.3 us)
Async XLA Ops:
  8.8 39.7 %copy-start = (s32[16384]{0:T(1024)S(1)}, s32[16384]{0:T(1024)}, u32[]{:S(2)}) copy-start(s32[16384]{0:T(1024)} %param.6) | copy-start | bytes 196612
  8.8 39.7 %copy-start.1 = (s32[256]{0:T(256)S(1)}, s32[256]{0:T(256)}, u32[]{:S(2)}) copy-start(s32[256]{0:T(256)} %param.7) | copy-start | bytes 3076
  21.4 26.1 %all-to-all-start = ((bf16[2,48,4,1024]{3,2,0,1:T(4,128)(2,1)}), bf16[2,48,4,1024]{3,2,0,1:T(4,128)(2,1)S(1)}, u32[]{:S(2)}, u32[]{:S(2)}) async-start(bf16[2,48,4,1024]{3,2,0,1:T(4,128)(2,1)} %copy.9), calls=%async_computation | async-start | bytes 1572864 | tf_op jit(solution)/shard_map/all_to_all | solution.py:57
  28.8 332.8 %reduce-scatter.4.cloned.1.call-start = ((), (), s32[]{:S(2)}) async-start(), calls=%async_computation.2 | async-start | bytes 139264
  304.7 58.2 %copy-start.2 = (f32[3,2,4,256]{3,2,1,0:T(4,128)}, f32[3,2,4,256]{3,2,1,0:T(4,128)S(1)}, u32[]{:S(2)}) copy-start(f32[3,2,4,256]{3,2,1,0:T(4,128)S(1)} %get-tuple-element.90) | copy-start | bytes 73732
Sparse Core Ops, SparseCore 0:
  305.7 55.8 reduce-scatter.3
where the time goes:
time: 370 us
  other arithmetic  204 us (55%)
  waiting for transfers between devices  74.7 us (20%)
  matrix products  54.4 us (15%)
  between operations  14.1 us (4%)
  loops' own time  7.92 us (2%)
  starting transfers between devices  7.43 us (2%)
  local copies, waits for them, and re-layouts  7.09 us (2%)
    cos x3, other arithmetic, make_phases(): return jnp.concatenate([jnp.cos(angles), jnp.sin(angles)], axis=1)  202 us
    unnamed x2, waiting for transfers between devices  56 us
    dot_general x6, matrix products, dedisperse(): jnp.dot(rows_wide, phases, precision=lax.Precision.HIGHEST, preferred_ele...  43.3 us
    all_to_all x1, waiting for transfers between devices, per_device(): lax.all_to_all(spectrum, 'chan', split_axis=1, concat_axis=3, tiled=True)  18.6 us
    dot_general x1, matrix products, per_device(): lax.dot_general(dft_table, voltages, (((0,), (2,)), ((), ())), preferred_...  11.1 us
    another operation x1, loops' own time, per_device(): spectra = lax.map(one_bin, jnp.arange(SPIN_DEV, dtype=jnp.int32))  7.92 us
  transfers between devices with their start and end apart: 2, of which 2 were waited for; matrix products, arithmetic and copies ran while one was open for 0% of the time, Pallas kernels for 0%

commit v1 on v0

--- a/solution.py
+++ b/solution.py
@@ -6,6 +6,23 @@
 
 SUBSTEPS = 512
 SPIN_DEV = 3
+
+
+def fill_tiles_here(d_out, my_data, net_axis, pos_dim):
+    mat_out = lax.axis_size(net_axis)
+    res, response = (mat_out, lax.axis_index(net_axis))
+    shaped = my_data.shape[pos_dim] // res
+    val = list(my_data.shape)
+    val[pos_dim] = shaped
+    out_arr = val[d_out]
+    val[d_out] = out_arr * res
+    ready = jnp.zeros(val, my_data.dtype)
+    for b in [*range(res)]:
+        back = lax.dynamic_slice_in_dim(my_data, (response ^ b) * shaped, shaped, axis=pos_dim)
+        if b:
+            back = lax.ppermute(back, net_axis, perm=[(h, h ^ b) for h in range(res)])
+        ready = lax.dynamic_update_slice_in_dim(ready, back, (response ^ b) * out_arr, axis=d_out)
+    return ready
 
 
 def build_table(samples, bins):
@@ -54,7 +71,7 @@
     )
     spectrum = (spectrum * (1.0 / math.sqrt(samples))).astype(jnp.bfloat16)
     spectrum = spectrum.reshape(2, bins_total, beam_count, local_chan)
-    regrouped = lax.all_to_all(spectrum, "chan", split_axis=1, concat_axis=3, tiled=True)
+    regrouped = fill_tiles_here(3, spectrum, "chan", 1)
     first_bin = lax.axis_index("chan") * SPIN_DEV
 
     def one_bin(offset):

time: 370 us -> 373 us (level)
  starting transfers between devices: 7.43 us -> 23.2 us
  waiting for transfers between devices: 74.7 us -> 60.7 us
    ppermute x0 -> x15, starting transfers between devices: none -> 23.1 us  [fill_tiles_here(): back = lax.ppermute(back, net_axis, perm=[(h, h ^ b) for h in range(res)])]
    all_to_all x1 -> x0, waiting for transfers between devices: 18.6 us -> none  [per_device(): lax.all_to_all(spectrum, 'chan', split_axis=1, concat_axis=3, tiled=True)]
    all_to_all x1 -> x0, starting transfers between devices: 7.39 us -> none  [per_device(): lax.all_to_all(spectrum, 'chan', split_axis=1, concat_axis=3, tiled=True)]
    ppermute x0 -> x15, waiting for transfers between devices: none -> 6.09 us  [fill_tiles_here(): back = lax.ppermute(back, net_axis, perm=[(h, h ^ b) for h in range(res)])]
  transfers between devices with their start and end apart: 2 -> 16, of which waited for: 2 -> 4; matrix products, arithmetic and copies ran while one was open for 0% -> 0% of each run, Pallas kernels for 0% -> 0%
where the time goes in v1:
time: 373 us; the launch traced here: 372 us
  other arithmetic  204 us (55%)
  waiting for transfers between devices  60.7 us (16%)
  matrix products  54.4 us (15%)
  starting transfers between devices  23.2 us (6%)
  between operations  14.7 us (4%)
  loops' own time  7.88 us (2%)
  local copies, waits for them, and re-layouts  7.45 us (2%)
    cos x3, other arithmetic, make_phases(): return jnp.concatenate([jnp.cos(angles), jnp.sin(angles)], axis=1)  202 us
    unnamed x2, waiting for transfers between devices  54.6 us
    dot_general x6, matrix products, dedisperse(): jnp.dot(rows_wide, phases, precision=lax.Precision.HIGHEST, preferred_ele...  43.3 us
    ppermute x15, starting transfers between devices, fill_tiles_here(): back = lax.ppermute(back, net_axis, perm=[(h, h ^ b) for h in range(res)])  23.1 us
    dot_general x1, matrix products, per_device(): lax.dot_general(dft_table, voltages, (((0,), (2,)), ((), ())), preferred_...  11.1 us
    another operation x1, loops' own time, per_device(): spectra = lax.map(one_bin, jnp.arange(SPIN_DEV, dtype=jnp.int32))  7.88 us
  transfers between devices with their start and end apart: 16, of which 4 were waited for; matrix products, arithmetic and copies ran while one was open for 0% of the time, Pallas kernels for 0%

profile of v1, /device:TPU:0, one launch (start us, length us, event | category | flops | bytes accessed | tf_op | source)
XLA Modules:
  0.0 372.4 jit_solution(783669077388918906)
XLA Ops:
  7.3 1.6 negate_convert_fusion
  9.0 11.1 %multiply_convert_fusion = bf16[96,4,1024]{2,0,1:T(8,128)(2,1)S(1)} fusion(bf16[4,1024,2048]{2,1,0:T(8,128)(2,1)} %param.5, bf16[2048,48]{0,1:T(8,128)(2,1)S(1)} %get-tuple-element.137, bf16[2048,48]{0,1:T(8,128)(2,1)S(1)} %get-tuple-element.138), kind=kOutput, calls=%fused_computation.47 | convolution fusion | flops 1612185600 | bytes 17956864 | tf_op jit(solution)/shard_map/dot_general | solution.py:69
  20.1 1.4 constant_dynamic-slice_fusion.1
  21.5 0.1 copy.40
  21.5 0.5 collective-permute-start
  22.1 2.6 collective-permute-start.1
  24.7 0.2 collective-permute-start.2
  25.0 1.8 collective-permute-start.3
  26.9 0.1 collective-permute-start.4
  27.0 0.2 broadcast_in_dim.6
  27.2 0.1 copy_dynamic-update-slice_fusion
  27.3 0.1 copy.45
  27.4 0.1 copy.46
  28.0 2.7 collective-permute-start.5
  30.7 0.2 collective-permute-start.6
  30.9 2.7 collective-permute-start.7
  33.7 0.1 collective-permute-start.8
  33.8 3.5 collective-permute-start.9
  37.4 0.2 collective-permute-start.10
  37.6 3.6 collective-permute-start.11
  41.3 0.1 collective-permute-start.12
  41.4 4.4 %collective-permute-start.13 = (bf16[2,3,4,1024]{3,2,1,0:T(4,128)(2,1)S(1)}, bf16[2,3,4,1024]{3,2,1,0:T(4,128)(2,1)S(1)}, u32[]{:S(2)}, u32[]{:S(2)}) collective-permute-start(bf16[2,3,4,1024]{3,2,1,0:T(4,128)(2,1)S(1)} %copy.53), channel_id=1, source_target_pairs={{0,14},{1,15},{2,12},{3,13},{4,10},{5,11},{6,8},{7,9},{8,6},{9,7},... | collective-permute-start | bytes 147464 | tf_op jit(solution)/shard_map/ppermute | solution.py:23
  45.9 0.4 collective-permute-start.14
  46.4 0.7 collective-permute-done.12
  47.1 2.2 collective-permute-done.13
  49.3 3.2 collective-permute-done.14
  52.6 256.2 %while.12 = (s32[]{:T(128)}, f32[3,2,4,256]{3,2,1,0:T(4,128)S(1)}, s32[3]{0:T(128)S(1)}, bf16[2,3,4,16384]{3,2,1,0:T(4,128)(2,1)S(1)}, s32[]{:T(128)}, /*index=5...) while((s32[]{:T(128)}, f32[3,2,4,256]{3,2,1,0:T(4,128)S(1)}, s32[3]{0:T(128)S(1)}, ...), condition=%wide.region_1.2_spmd, body=%wide.region_0.1_spmd.sunk | while | flops 872620032 | bytes 68955304 | solution.py:85
  52.7 0.7 dynamic_slice.98
  55.3 0.1 constant_dynamic-slice_fusion.18
  55.4 0.1 reshape.66
  56.1 67.4 %fusion.55 = (f32[16384,128]{1,0:T(8,128)S(1)}, f32[16384,128]{1,0:T(8,128)S(1)}, f32[16384,128]{1,0:T(8,128)}, f32[16384,128]{1,0:T(8,128)}) fusion(s32[128]{0:T(128)S(1)} %get-tuple-element.194, s32[16384]{0:T(1024)S(1)} %add_select_fusion.5, s32[128]{0:T(128)S(1)} %get-tuple-element.195), kind=kLoop, calls=%fused_computation.27.clone.1 | loop fusion | flops 58720256 | bytes 33620992 | tf_op jit(solution)/shard_map/while/body/eval_jaxpr/cos | solution.py:40
  123.6 8.9 %fusion.58 = f32[8,256]{1,0:T(8,128)S(1)} fusion(bf16[8,16384]{1,0:T(8,128)(2,1)S(1)} %reshape.66, f32[16384,128]{1,0:T(8,128)} %get-tuple-element.200, f32[16384,128]{1,0:T(8,128)} %get-tuple-element.201), kind=kOutput, calls=%fused_computation.4.clone.1 | convolution fusion | flops 406847488 | bytes 17047552 | tf_op jit(solution)/shard_map/while/body/eval_jaxpr/dot_general | solution.py:50
  132.5 5.5 %fusion.56 = f32[8,256]{1,0:T(8,128)S(1)} fusion(bf16[8,16384]{1,0:T(8,128)(2,1)S(1)} %reshape.66, f32[16384,128]{1,0:T(8,128)S(1)} %get-tuple-element.196, f32[16384,128]{1,0:T(8,128)S(1)} %get-tuple-element.197), kind=kOutput, calls=%fused_computation.clone.1 | convolution fusion | flops 406847488 | bytes 17047552 | tf_op jit(solution)/shard_map/while/body/eval_jaxpr/dot_general | solution.py:50
  138.1 0.7 dynamic_slice.98
  140.6 0.1 constant_dynamic-slice_fusion.18
  140.7 0.1 reshape.66
  141.5 67.4 %fusion.55 = (f32[16384,128]{1,0:T(8,128)S(1)}, f32[16384,128]{1,0:T(8,128)S(1)}, f32[16384,128]{1,0:T(8,128)}, f32[16384,128]{1,0:T(8,128)}) fusion(s32[128]{0:T(128)S(1)} %get-tuple-element.194, s32[16384]{0:T(1024)S(1)} %add_select_fusion.5, s32[128]{0:T(128)S(1)} %get-tuple-element.195), kind=kLoop, calls=%fused_computation.27.clone.1 | loop fusion | flops 58720256 | bytes 33620992 | tf_op jit(solution)/shard_map/while/body/eval_jaxpr/cos | solution.py:40
  208.9 8.9 %fusion.58 = f32[8,256]{1,0:T(8,128)S(1)} fusion(bf16[8,16384]{1,0:T(8,128)(2,1)S(1)} %reshape.66, f32[16384,128]{1,0:T(8,128)} %get-tuple-element.200, f32[16384,128]{1,0:T(8,128)} %get-tuple-element.201), kind=kOutput, calls=%fused_computation.4.clone.1 | convolution fusion | flops 406847488 | bytes 17047552 | tf_op jit(solution)/shard_map/while/body/eval_jaxpr/dot_general | solution.py:50
  217.8 5.5 %fusion.56 = f32[8,256]{1,0:T(8,128)S(1)} fusion(bf16[8,16384]{1,0:T(8,128)(2,1)S(1)} %reshape.66, f32[16384,128]{1,0:T(8,128)S(1)} %get-tuple-element.196, f32[16384,128]{1,0:T(8,128)S(1)} %get-tuple-element.197), kind=kOutput, calls=%fused_computation.clone.1 | convolution fusion | flops 406847488 | bytes 17047552 | tf_op jit(solution)/shard_map/while/body/eval_jaxpr/dot_general | solution.py:50
  223.4 0.7 dynamic_slice.98
  226.0 0.1 constant_dynamic-slice_fusion.18
  226.1 0.1 reshape.66
  226.8 67.4 %fusion.55 = (f32[16384,128]{1,0:T(8,128)S(1)}, f32[16384,128]{1,0:T(8,128)S(1)}, f32[16384,128]{1,0:T(8,128)}, f32[16384,128]{1,0:T(8,128)}) fusion(s32[128]{0:T(128)S(1)} %get-tuple-element.194, s32[16384]{0:T(1024)S(1)} %add_select_fusion.5, s32[128]{0:T(128)S(1)} %get-tuple-element.195), kind=kLoop, calls=%fused_computation.27.clone.1 | loop fusion | flops 58720256 | bytes 33620992 | tf_op jit(solution)/shard_map/while/body/eval_jaxpr/cos | solution.py:40
  294.3 8.9 %fusion.58 = f32[8,256]{1,0:T(8,128)S(1)} fusion(bf16[8,16384]{1,0:T(8,128)(2,1)S(1)} %reshape.66, f32[16384,128]{1,0:T(8,128)} %get-tuple-element.200, f32[16384,128]{1,0:T(8,128)} %get-tuple-element.201), kind=kOutput, calls=%fused_computation.4.clone.1 | convolution fusion | flops 406847488 | bytes 17047552 | tf_op jit(solution)/shard_map/while/body/eval_jaxpr/dot_general | solution.py:50
  303.2 5.5 %fusion.56 = f32[8,256]{1,0:T(8,128)S(1)} fusion(bf16[8,16384]{1,0:T(8,128)(2,1)S(1)} %reshape.66, f32[16384,128]{1,0:T(8,128)S(1)} %get-tuple-element.196, f32[16384,128]{1,0:T(8,128)S(1)} %get-tuple-element.197), kind=kOutput, calls=%fused_computation.clone.1 | convolution fusion | flops 406847488 | bytes 17047552 | tf_op jit(solution)/shard_map/while/body/eval_jaxpr/dot_general | solution.py:50
  308.8 0.8 copy.37
  309.6 54.6 %reduce-scatter.4.cloned.1.call-done = f32[16,4]{1,0:T(8,128)} async-done(((f32[256,4]{1,0:T(8,128)}), f32[16,4]{1,0:T(8,128)}) %reduce-scatter.4.cloned.1.call-update) | async-done | bytes 272
  364.2 1.3 copy.38
  (69 shorter events, 1.4 us)
Async XLA Ops:
  7.2 357.1 %reduce-scatter.4.cloned.1.call-start = ((), (), s32[]{:S(2)}) async-start(), calls=%async_computation.1 | async-start | bytes 139264
  9.0 43.5 %copy-start = (s32[16384]{0:T(1024)S(1)}, s32[16384]{0:T(1024)}, u32[]{:S(2)}) copy-start(s32[16384]{0:T(1024)} %param.6) | copy-start | bytes 196612
  9.0 43.5 %copy-start.1 = (s32[256]{0:T(256)S(1)}, s32[256]{0:T(256)}, u32[]{:S(2)}) copy-start(s32[256]{0:T(256)} %param.7) | copy-start | bytes 3076
  21.5 6.4 %collective-permute-start = (bf16[2,3,4,1024]{3,2,1,0:T(4,128)(2,1)S(1)}, bf16[2,3,4,1024]{3,2,1,0:T(4,128)(2,1)S(1)}, u32[]{:S(2)}, u32[]{:S(2)}) collective-permute-start(bf16[2,3,4,1024]{3,2,1,0:T(4,128)(2,1)S(1)} %copy.40), channel_id=1, source_target_pairs={{0,1},{1,0},{2,3},{3,2},{4,5},{5,4},{6,7},{7,6},{8,9},{9,8},{10,11... | collective-permute-start | bytes 147464 | tf_op jit(solution)/shard_map/ppermute | solution.py:23
  22.1 8.6 %collective-permute-start.1 = (bf16[2,3,4,1024]{3,2,1,0:T(4,128)(2,1)S(1)}, bf16[2,3,4,1024]{3,2,1,0:T(4,128)(2,1)S(1)}, u32[]{:S(2)}, u32[]{:S(2)}) collective-permute-start(bf16[2,3,4,1024]{3,2,1,0:T(4,128)(2,1)S(1)} %copy.41), channel_id=1, source_target_pairs={{0,2},{1,3},{2,0},{3,1},{4,6},{5,7},{6,4},{7,5},{8,10},{9,11},{10,... | collective-permute-start | bytes 147464 | tf_op jit(solution)/shard_map/ppermute | solution.py:23
  24.7 6.1 %collective-permute-start.2 = (bf16[2,3,4,1024]{3,2,1,0:T(4,128)(2,1)S(1)}, bf16[2,3,4,1024]{3,2,1,0:T(4,128)(2,1)S(1)}, u32[]{:S(2)}, u32[]{:S(2)}) collective-permute-start(bf16[2,3,4,1024]{3,2,1,0:T(4,128)(2,1)S(1)} %copy.42), channel_id=1, source_target_pairs={{0,3},{1,2},{2,1},{3,0},{4,7},{5,6},{6,5},{7,4},{8,11},{9,10},{10,... | collective-permute-start | bytes 147464 | tf_op jit(solution)/shard_map/ppermute | solution.py:23
  25.0 8.7 %collective-permute-start.3 = (bf16[2,3,4,1024]{3,2,1,0:T(4,128)(2,1)S(1)}, bf16[2,3,4,1024]{3,2,1,0:T(4,128)(2,1)S(1)}, u32[]{:S(2)}, u32[]{:S(2)}) collective-permute-start(bf16[2,3,4,1024]{3,2,1,0:T(4,128)(2,1)S(1)} %copy.43), channel_id=1, source_target_pairs={{0,4},{1,5},{2,6},{3,7},{4,0},{5,1},{6,2},{7,3},{8,12},{9,13},{10,... | collective-permute-start | bytes 147464 | tf_op jit(solution)/shard_map/ppermute | solution.py:23
  26.9 6.9 %collective-permute-start.4 = (bf16[2,3,4,1024]{3,2,1,0:T(4,128)(2,1)S(1)}, bf16[2,3,4,1024]{3,2,1,0:T(4,128)(2,1)S(1)}, u32[]{:S(2)}, u32[]{:S(2)}) collective-permute-start(bf16[2,3,4,1024]{3,2,1,0:T(4,128)(2,1)S(1)} %copy.44), channel_id=1, source_target_pairs={{0,5},{1,4},{2,7},{3,6},{4,1},{5,0},{6,3},{7,2},{8,13},{9,12},{10,... | collective-permute-start | bytes 147464 | tf_op jit(solution)/shard_map/ppermute | solution.py:23
  28.0 9.4 %collective-permute-start.5 = (bf16[2,3,4,1024]{3,2,1,0:T(4,128)(2,1)S(1)}, bf16[2,3,4,1024]{3,2,1,0:T(4,128)(2,1)S(1)}, u32[]{:S(2)}, u32[]{:S(2)}) collective-permute-start(bf16[2,3,4,1024]{3,2,1,0:T(4,128)(2,1)S(1)} %copy.45), channel_id=1, source_target_pairs={{0,6},{1,7},{2,4},{3,5},{4,2},{5,3},{6,0},{7,1},{8,14},{9,15},{10,... | collective-permute-start | bytes 147464 | tf_op jit(solution)/shard_map/ppermute | solution.py:23
  30.7 6.9 %collective-permute-start.6 = (bf16[2,3,4,1024]{3,2,1,0:T(4,128)(2,1)S(1)}, bf16[2,3,4,1024]{3,2,1,0:T(4,128)(2,1)S(1)}, u32[]{:S(2)}, u32[]{:S(2)}) collective-permute-start(bf16[2,3,4,1024]{3,2,1,0:T(4,128)(2,1)S(1)} %copy.46), channel_id=1, source_target_pairs={{0,7},{1,6},{2,5},{3,4},{4,3},{5,2},{6,1},{7,0},{8,15},{9,14},{10,... | collective-permute-start | bytes 147464 | tf_op jit(solution)/shard_map/ppermute | solution.py:23
  30.9 10.4 %collective-permute-start.7 = (bf16[2,3,4,1024]{3,2,1,0:T(4,128)(2,1)S(1)}, bf16[2,3,4,1024]{3,2,1,0:T(4,128)(2,1)S(1)}, u32[]{:S(2)}, u32[]{:S(2)}) collective-permute-start(bf16[2,3,4,1024]{3,2,1,0:T(4,128)(2,1)S(1)} %copy.47), channel_id=1, source_target_pairs={{0,8},{1,9},{2,10},{3,11},{4,12},{5,13},{6,14},{7,15},{8,0},{9,1},... | collective-permute-start | bytes 147464 | tf_op jit(solution)/shard_map/ppermute | solution.py:23
  33.7 7.7 %collective-permute-start.8 = (bf16[2,3,4,1024]{3,2,1,0:T(4,128)(2,1)S(1)}, bf16[2,3,4,1024]{3,2,1,0:T(4,128)(2,1)S(1)}, u32[]{:S(2)}, u32[]{:S(2)}) collective-permute-start(bf16[2,3,4,1024]{3,2,1,0:T(4,128)(2,1)S(1)} %copy.48), channel_id=1, source_target_pairs={{0,9},{1,8},{2,11},{3,10},{4,13},{5,12},{6,15},{7,14},{8,1},{9,0},... | collective-permute-start | bytes 147464 | tf_op jit(solution)/shard_map/ppermute | solution.py:23
  33.8 12.1 %collective-permute-start.9 = (bf16[2,3,4,1024]{3,2,1,0:T(4,128)(2,1)S(1)}, bf16[2,3,4,1024]{3,2,1,0:T(4,128)(2,1)S(1)}, u32[]{:S(2)}, u32[]{:S(2)}) collective-permute-start(bf16[2,3,4,1024]{3,2,1,0:T(4,128)(2,1)S(1)} %copy.49), channel_id=1, source_target_pairs={{0,10},{1,11},{2,8},{3,9},{4,14},{5,15},{6,12},{7,13},{8,2},{9,3},... | collective-permute-start | bytes 147464 | tf_op jit(solution)/shard_map/ppermute | solution.py:23
  37.4 8.9 %collective-permute-start.10 = (bf16[2,3,4,1024]{3,2,1,0:T(4,128)(2,1)S(1)}, bf16[2,3,4,1024]{3,2,1,0:T(4,128)(2,1)S(1)}, u32[]{:S(2)}, u32[]{:S(2)}) collective-permute-start(bf16[2,3,4,1024]{3,2,1,0:T(4,128)(2,1)S(1)} %copy.50), channel_id=1, source_target_pairs={{0,11},{1,10},{2,9},{3,8},{4,15},{5,14},{6,13},{7,12},{8,3},{9,2},... | collective-permute-start | bytes 147464 | tf_op jit(solution)/shard_map/ppermute | solution.py:23
  37.6 8.7 %collective-permute-start.11 = (bf16[2,3,4,1024]{3,2,1,0:T(4,128)(2,1)S(1)}, bf16[2,3,4,1024]{3,2,1,0:T(4,128)(2,1)S(1)}, u32[]{:S(2)}, u32[]{:S(2)}) collective-permute-start(bf16[2,3,4,1024]{3,2,1,0:T(4,128)(2,1)S(1)} %copy.51), channel_id=1, source_target_pairs={{0,12},{1,13},{2,14},{3,15},{4,8},{5,9},{6,10},{7,11},{8,4},{9,5},... | collective-permute-start | bytes 147464 | tf_op jit(solution)/shard_map/ppermute | solution.py:23
  41.3 5.8 %collective-permute-start.12 = (bf16[2,3,4,1024]{3,2,1,0:T(4,128)(2,1)S(1)}, bf16[2,3,4,1024]{3,2,1,0:T(4,128)(2,1)S(1)}, u32[]{:S(2)}, u32[]{:S(2)}) collective-permute-start(bf16[2,3,4,1024]{3,2,1,0:T(4,128)(2,1)S(1)} %copy.52), channel_id=1, source_target_pairs={{0,13},{1,12},{2,15},{3,14},{4,9},{5,8},{6,11},{7,10},{8,5},{9,4},... | collective-permute-start | bytes 147464 | tf_op jit(solution)/shard_map/ppermute | solution.py:23
  41.4 7.9 %collective-permute-start.13 = (bf16[2,3,4,1024]{3,2,1,0:T(4,128)(2,1)S(1)}, bf16[2,3,4,1024]{3,2,1,0:T(4,128)(2,1)S(1)}, u32[]{:S(2)}, u32[]{:S(2)}) collective-permute-start(bf16[2,3,4,1024]{3,2,1,0:T(4,128)(2,1)S(1)} %copy.53), channel_id=1, source_target_pairs={{0,14},{1,15},{2,12},{3,13},{4,10},{5,11},{6,8},{7,9},{8,6},{9,7},... | collective-permute-start | bytes 147464 | tf_op jit(solution)/shard_map/ppermute | solution.py:23
  45.9 6.6 %collective-permute-start.14 = (bf16[2,3,4,1024]{3,2,1,0:T(4,128)(2,1)S(1)}, bf16[2,3,4,1024]{3,2,1,0:T(4,128)(2,1)S(1)}, u32[]{:S(2)}, u32[]{:S(2)}) collective-permute-start(bf16[2,3,4,1024]{3,2,1,0:T(4,128)(2,1)S(1)} %copy.54), channel_id=1, source_target_pairs={{0,15},{1,14},{2,13},{3,12},{4,11},{5,10},{6,9},{7,8},{8,7},{9,6},... | collective-permute-start | bytes 147464 | tf_op jit(solution)/shard_map/ppermute | solution.py:23
  308.8 56.8 %copy-start.2 = (f32[3,2,4,256]{3,2,1,0:T(4,128)}, f32[3,2,4,256]{3,2,1,0:T(4,128)S(1)}, u32[]{:S(2)}) copy-start(f32[3,2,4,256]{3,2,1,0:T(4,128)S(1)} %get-tuple-element.90) | copy-start | bytes 73732
Sparse Core Ops, SparseCore 0:
  309.8 54.4 reduce-scatter.3
